TPU v7x, 32 devices: a whole 2x2x4 slice. The times are simulated.
32 devices in a mesh: loop: 4 (over x, core), grp: 8 (over z, y).
Axes of the slice: x: 2, y: 2, z: 4, core: 2. Of those that a mesh axis runs over, the one named last changes fastest.
Arguments:
- basis: bfloat16 [24576, 256], P(('loop', 'grp')), may hold values from -6 to 6
- stiffness: bfloat16 [384, 16, 4096], P(('loop', 'grp')), may hold values from -0.1875 to 0.1875
- mass: bfloat16 [384, 16, 4096], P(('loop', 'grp')), may hold values from -0.1875 to 0.1875
- col_index: int32 [384, 16], P(('loop', 'grp')), may hold values from 0 to 11
- live_counts: int32 [384], P(('loop', 'grp')), may hold values from 1 to 16, as said below
Outputs:
- stiff_basis: bfloat16 [24576, 256], P(('loop', 'grp'))
- mass_basis: bfloat16 [24576, 256], P(('loop', 'grp'))
- stiff_gram: float32 [256, 256], replicated
- mass_gram: float32 [256, 256], replicated
Inputs may be any that keep to these rules, and one draw needn't show every extreme that they name: `live_counts`: every block row keeps at least one block; some block row uses all 16 and some only one.
All inputs are finite; a program needn't handle non-finite values.
Results may differ from a plain program's by a relative error of at most 0.0029.
Values may be sent and summed in bfloat16 or wider, within the bound.
A program may use at most 64 MiB of HBM per device.

v0:
```python
import jax
import jax.numpy as jnp
from jax import lax
from jax.sharding import PartitionSpec as P

BS = 64
NB = 16
panel_spans = ((0, 0, 6), (1, 6, 3), (-1, 9, 3), (2, 12, 2), (-2, 14, 2))


def shifted(block, axis, distance):
    devices = range(lax.axis_size(axis))
    route = [((i - distance) % len(devices), i) for i in devices]
    return lax.ppermute(block, axis, route)


def on_device(basis, stiffness, mass, col_index, live_counts):
    rows_dev = stiffness.shape[0]
    width = basis.shape[1]
    kb = stiffness.reshape(rows_dev, NB, BS, BS)
    mb = mass.reshape(rows_dev, NB, BS, BS)
    slot_ids = jnp.arange(NB, dtype=jnp.int32)
    live_grid = slot_ids[None, :] < live_counts[:, None]
    panels = {
        0: basis,
        1: shifted(basis, "loop", -1),
        -1: shifted(basis, "loop", 1),
        2: shifted(basis, "loop", -2),
        -2: shifted(basis, "loop", 2),
    }
    zeros_acc = jnp.zeros((rows_dev, BS, width), jnp.float32)
    accs = (zeros_acc, zeros_acc)
    for shift_by, first, count in panel_spans:
        blocks = panels[shift_by].reshape(rows_dev, BS, width)
        chosen = col_index[:, first : first + count]
        alive = live_grid[:, first : first + count]
        picked = blocks[chosen]
        picked = jnp.where(alive[:, :, None, None], picked, jnp.zeros_like(picked))
        kadd = jnp.einsum(
            "rjab,rjbc->rac",
            kb[:, first : first + count],
            picked,
            preferred_element_type=jnp.float32,
        )
        madd = jnp.einsum(
            "rjab,rjbc->rac",
            mb[:, first : first + count],
            picked,
            preferred_element_type=jnp.float32,
        )
        accs = (accs[0] + kadd, accs[1] + madd)
    kacc, macc = accs
    stiff_basis = kacc.reshape(rows_dev * BS, width).astype(jnp.bfloat16)
    mass_basis = macc.reshape(rows_dev * BS, width).astype(jnp.bfloat16)
    contract = (((0,), (0,)), ((), ()))
    kterm = lax.dot_general(basis, stiff_basis, contract, preferred_element_type=jnp.float32)
    mterm = lax.dot_general(basis, mass_basis, contract, preferred_element_type=jnp.float32)
    kgram, mgram = lax.psum((kterm, mterm), ("loop", "grp"))
    total_dofs = basis.shape[0] * lax.axis_size("loop") * lax.axis_size("grp")
    factor = jnp.float32(1.0) / jnp.sqrt(jnp.float32(total_dofs))
    return (stiff_basis, mass_basis, kgram * factor, mgram * factor)


def solution(mesh):
    in_specs = (
        P(("loop", "grp"), None),
        P(("loop", "grp"), None, None),
        P(("loop", "grp"), None, None),
        P(("loop", "grp"), None),
        P(("loop", "grp")),
    )
    out_specs = (P(("loop", "grp"), None), P(("loop", "grp"), None), P(), P())
    return jax.shard_map(
        on_device, mesh=mesh, in_specs=in_specs, out_specs=out_specs, check_vma=False
    )
```

profile of v0, /device:TPU:0, one launch (start us, length us, event | category | flops | bytes accessed | tf_op | source)
XLA Modules:
  0.0 197.9 jit_solution(3938690956162846545)
XLA Ops:
  7.2 0.0 all-reduce.3.cloned.1.call-start
  7.2 0.5 collective-permute-start.1
  7.7 2.0 %collective-permute-start = (bf16[768,256]{1,0:T(8,128)(2,1)}, bf16[768,256]{1,0:T(8,128)(2,1)}, u32[]{:S(2)}, u32[]{:S(2)}) collective-permute-start(bf16[768,256]{1,0:T(8,128)(2,1)} %param.5), channel_id=1, source_target_pairs={{8,0},{16,8},{24,16},{0,24},{9,1},{17,9},{25,17},{1,25},{10,2},{18... | collective-permute-start | bytes 1179656 | tf_op jit(solution)/shard_map/ppermute | solution.py:14
  9.7 2.2 %collective-permute-start.2 = (bf16[768,256]{1,0:T(8,128)(2,1)}, bf16[768,256]{1,0:T(8,128)(2,1)}, u32[]{:S(2)}, u32[]{:S(2)}) collective-permute-start(bf16[768,256]{1,0:T(8,128)(2,1)} %param.5), channel_id=1, source_target_pairs={{16,0},{24,8},{0,16},{8,24},{17,1},{25,9},{1,17},{9,25},{18,2},{26... | collective-permute-start | bytes 1179656 | tf_op jit(solution)/shard_map/ppermute | solution.py:14
  11.9 0.8 compare_select_fusion.3
  12.8 0.7 compare_select_fusion.4
  13.5 0.7 iota_compare_fusion
  14.2 0.7 fusion.35
  14.9 0.7 fusion.34
  15.5 0.8 compare_select_fusion.1
  16.4 4.3 %reshape.42 = bf16[12,16,64,64]{3,2,1,0:T(8,128)(2,1)S(1)} reshape(bf16[12,16,4096]{2,1,0:T(8,128)(2,1)} %param.7) | data formatting | bytes 3145728 | tf_op jit(solution)/shard_map/reshape | solution.py:21
  20.7 0.1 reshape.61
  20.8 0.1 reshape.45
  20.9 0.1 reshape.53
  21.0 0.1 reshape.77
  21.1 0.6 pad_clamp_fusion
  21.7 0.1 reshape.69
  21.8 0.6 pad_clamp_fusion.1
  22.4 5.5 %reshape.38 = bf16[12,16,64,64]{3,2,1,0:T(8,128)(2,1)} reshape(bf16[12,16,4096]{2,1,0:T(8,128)(2,1)} %param.6) | data formatting | bytes 3145728 | tf_op jit(solution)/shard_map/reshape | solution.py:20
  27.9 2.4 %gather_fusion = bf16[72,64,256]{2,1,0:T(8,128)(2,1)} fusion(bf16[12,64,256]{2,1,0:T(8,128)(2,1)S(1)} %bitcast.84, s32[1024]{0:T(1024)S(1)} %pad_clamp_fusion.4), kind=kCustom, calls=%fused_computation | custom fusion | bytes 4718880 | tf_op jit(solution)/shard_map/gather | solution.py:37
  30.3 3.3 %fusion.2 = f32[12,256,64]{1,2,0:T(8,128)} fusion(bf16[12,16,64,64]{3,2,1,0:T(8,128)(2,1)S(1)} %reshape.42, bf16[12,6,64,256]{3,2,1,0:T(8,128)(2,1)} %bitcast.91, pred[12,6]{1,0:T(8,128)(4,1)S(1)} %bitcast.99), kind=kOutput, calls=%fused_computation.8 | convolution fusion | flops 152174592 | bytes 4718664 | tf_op jit(solution)/shard_map/rjab,rjbc->rac/dot_general | solution.py:45
  33.6 1.5 fusion.3
  35.2 0.0 collective-permute-done.2
  35.2 2.6 %gather_fusion.4 = bf16[24,64,256]{2,1,0:T(8,128)(2,1)} fusion(bf16[12,64,256]{2,1,0:T(8,128)(2,1)} %bitcast.12, s32[1024]{0:T(1024)S(1)} %copy-done.15), kind=kCustom, calls=%fused_computation.4 | custom fusion | bytes 1572960 | tf_op jit(solution)/shard_map/gather | solution.py:37
  37.7 2.6 %gather_fusion.3 = bf16[24,64,256]{2,1,0:T(8,128)(2,1)} fusion(bf16[12,64,256]{2,1,0:T(8,128)(2,1)} %bitcast.12, s32[1024]{0:T(1024)} %pad_clamp_fusion.1), kind=kCustom, calls=%fused_computation.3 | custom fusion | bytes 1572960 | tf_op jit(solution)/shard_map/gather | solution.py:37
  40.3 0.0 collective-permute-done.1
  40.4 2.7 %gather_fusion.2 = bf16[36,64,256]{2,1,0:T(8,128)(2,1)} fusion(bf16[12,64,256]{2,1,0:T(8,128)(2,1)} %bitcast.8, s32[1024]{0:T(1024)S(1)} %pad_clamp_fusion.2), kind=kCustom, calls=%fused_computation.2 | custom fusion | bytes 2359440 | tf_op jit(solution)/shard_map/gather | solution.py:37
  43.1 2.7 %convolution_bitcast_fusion.4 = f32[12,256,64]{1,2,0:T(8,128)} fusion(bf16[12,16,64,64]{3,2,1,0:T(8,128)(2,1)S(1)} %reshape.42, bf16[12,3,64,256]{3,2,1,0:T(8,128)(2,1)} %bitcast.97, pred[12,3]{1,0:T(8,128)(4,1)S(1)} %copy-done.19), kind=kOutput, calls=%fused_computation.14 | convolution fusion | flops 76087296 | bytes 3538980 | tf_op jit(solution)/shard_map/rjab,rjbc->rac/dot_general | solution.py:45
  45.8 1.3 convolution_bitcast_fusion
  47.1 1.2 convolution_bitcast_fusion.2
  48.3 1.3 convolution_bitcast_fusion.6
  49.6 2.7 %gather_fusion.1 = bf16[36,64,256]{2,1,0:T(8,128)(2,1)} fusion(bf16[12,64,256]{2,1,0:T(8,128)(2,1)} %bitcast.4, s32[1024]{0:T(1024)S(1)} %pad_clamp_fusion.3), kind=kCustom, calls=%fused_computation.1 | custom fusion | bytes 2359440 | tf_op jit(solution)/shard_map/gather | solution.py:37
  52.4 2.3 %fusion.11 = f32[12,256,64]{1,2,0:T(8,128)S(1)} fusion(f32[12,256,64]{1,2,0:T(8,128)} %convolution_bitcast_fusion.4, f32[12,256,64]{1,2,0:T(8,128)} %fusion.2, bf16[12,16,64,64]{3,2,1,0:T(8,128)(2,1)S(1)} %reshape.42, bf16[12,3,64,256]{3,2,1,0:T(8,128)(2,1)} %bitcast.85, pred[12,3]{1,0:T(8,128)(4,1)S(1)} %copy-done.17), kind=kOutput, calls=%fused_computation.25 | convolution fusion | flops 76480512 | bytes 5111844 | tf_op jit(solution)/shard_map/rjab,rjbc->rac/dot_general | solution.py:45
  54.7 0.3 fusion.12
  55.1 0.0 copy-start.10
  55.1 1.0 convolution_bitcast_fusion.8
  56.1 0.8 copy-done.3
  56.9 0.3 copy-done.4
  57.2 0.4 fusion.9
  57.6 0.7 copy-done.7
  58.3 0.3 fusion.13
  58.7 0.0 copy-start.11
  58.7 1.0 convolution_bitcast_fusion.9
  59.7 0.0 all-reduce.3.cloned.1.call-update
  59.7 128.6 %all-reduce.3.cloned.1.call-done = (f32[256,256]{0,1:T(8,128)}, f32[256,256]{0,1:T(8,128)}) async-done(((f32[256,256]{0,1:T(8,128)}, f32[256,256]{0,1:T(8,128)}), (f32[256,256]{0,1:T(8,128)}, f32[256,256]{0,1:T(8,128)})) %all-reduce.3.cloned.1.call-update) | async-done | bytes 524304 | tf_op jit(solution)/shard_map/psum | solution.py:58
  188.3 1.1 broadcast_multiply_fusion
  189.4 0.8 copy.11
  190.2 0.8 copy.12
  (39 shorter events, 0.1 us)
Async XLA Ops:
  7.2 181.1 %all-reduce.3.cloned.1.call-start = ((), (), s32[]{:S(2)}) async-start(), calls=%async_computation | async-start | bytes 1048576 | tf_op jit(solution)/shard_map/psum | solution.py:58
  7.2 33.1 %collective-permute-start.1 = (bf16[768,256]{1,0:T(8,128)(2,1)}, bf16[768,256]{1,0:T(8,128)(2,1)}, u32[]{:S(2)}, u32[]{:S(2)}) collective-permute-start(bf16[768,256]{1,0:T(8,128)(2,1)} %param.5), channel_id=1, source_target_pairs={{24,0},{0,8},{8,16},{16,24},{25,1},{1,9},{9,17},{17,25},{26,2},{2,... | collective-permute-start | bytes 1179656 | tf_op jit(solution)/shard_map/ppermute | solution.py:14
  7.7 41.9 %collective-permute-start = (bf16[768,256]{1,0:T(8,128)(2,1)}, bf16[768,256]{1,0:T(8,128)(2,1)}, u32[]{:S(2)}, u32[]{:S(2)}) collective-permute-start(bf16[768,256]{1,0:T(8,128)(2,1)} %param.5), channel_id=1, source_target_pairs={{8,0},{16,8},{24,16},{0,24},{9,1},{17,9},{25,17},{1,25},{10,2},{18... | collective-permute-start | bytes 1179656 | tf_op jit(solution)/shard_map/ppermute | solution.py:14
  9.7 25.5 %collective-permute-start.2 = (bf16[768,256]{1,0:T(8,128)(2,1)}, bf16[768,256]{1,0:T(8,128)(2,1)}, u32[]{:S(2)}, u32[]{:S(2)}) collective-permute-start(bf16[768,256]{1,0:T(8,128)(2,1)} %param.5), channel_id=1, source_target_pairs={{16,0},{24,8},{0,16},{8,24},{17,1},{25,9},{1,17},{9,25},{18,2},{26... | collective-permute-start | bytes 1179656 | tf_op jit(solution)/shard_map/ppermute | solution.py:14
  22.4 5.5 %copy-start = (bf16[768,256]{1,0:T(8,128)(2,1)S(1)}, bf16[768,256]{1,0:T(8,128)(2,1)}, u32[]{:S(2)}) copy-start(bf16[768,256]{1,0:T(8,128)(2,1)} %param.5) | copy-start | bytes 1179652
  30.3 3.3 %copy-start.1 = (bf16[12,16,64,64]{3,2,1,0:T(8,128)(2,1)S(1)}, bf16[12,16,64,64]{3,2,1,0:T(8,128)(2,1)}, u32[]{:S(2)}) copy-start(bf16[12,16,64,64]{3,2,1,0:T(8,128)(2,1)} %reshape.38) | copy-start | bytes 4718596
  30.3 3.3 %copy-start.9 = (bf16[72,64,256]{2,1,0:T(8,128)(2,1)S(1)}, bf16[72,64,256]{2,1,0:T(8,128)(2,1)}, u32[]{:S(2)}) copy-start(bf16[72,64,256]{2,1,0:T(8,128)(2,1)} %gather_fusion) | copy-start | bytes 7077892
  33.6 1.5 copy-start.15
  37.7 5.4 %copy-start.19 = (pred[12,3]{1,0:T(8,128)(4,1)S(1)}, pred[12,3]{1,0:T(8,128)(4,1)}, u32[]{:S(2)}) copy-start(pred[12,3]{1,0:T(8,128)(4,1)} %get-tuple-element.21) | copy-start | bytes 112
  40.4 5.5 %copy-start.18 = (pred[12,2]{1,0:T(8,128)(4,1)S(1)}, pred[12,2]{1,0:T(8,128)(4,1)}, u32[]{:S(2)}) copy-start(pred[12,2]{1,0:T(8,128)(4,1)} %get-tuple-element.19) | copy-start | bytes 76
  43.1 2.7 %copy-start.6 = (bf16[24,64,256]{2,1,0:T(8,128)(2,1)S(1)}, bf16[24,64,256]{2,1,0:T(8,128)(2,1)}, u32[]{:S(2)}) copy-start(bf16[24,64,256]{2,1,0:T(8,128)(2,1)} %gather_fusion.4) | copy-start | bytes 2359300
  43.1 4.0 %copy-start.2 = (bf16[12,16,64,64]{3,2,1,0:T(8,128)(2,1)S(1)}, bf16[12,16,64,64]{3,2,1,0:T(8,128)(2,1)}, u32[]{:S(2)}) copy-start(bf16[12,16,64,64]{3,2,1,0:T(8,128)(2,1)} %reshape.38) | copy-start | bytes 4718596
  45.8 2.5 %copy-start.12 = (bf16[36,64,256]{2,1,0:T(8,128)(2,1)S(1)}, bf16[36,64,256]{2,1,0:T(8,128)(2,1)}, u32[]{:S(2)}) copy-start(bf16[36,64,256]{2,1,0:T(8,128)(2,1)} %gather_fusion.2) | copy-start | bytes 3538948
  48.3 4.0 %copy-start.17 = (pred[12,3]{1,0:T(8,128)(4,1)S(1)}, pred[12,3]{1,0:T(8,128)(4,1)}, u32[]{:S(2)}) copy-start(pred[12,3]{1,0:T(8,128)(4,1)} %get-tuple-element.20) | copy-start | bytes 112
  52.4 2.3 %copy-start.5 = (bf16[24,64,256]{2,1,0:T(8,128)(2,1)S(1)}, bf16[24,64,256]{2,1,0:T(8,128)(2,1)}, u32[]{:S(2)}) copy-start(bf16[24,64,256]{2,1,0:T(8,128)(2,1)} %gather_fusion.3) | copy-start | bytes 2359300
  52.4 2.3 %copy-start.8 = (f32[12,256,64]{1,2,0:T(8,128)S(1)}, f32[12,256,64]{1,2,0:T(8,128)}, u32[]{:S(2)}) copy-start(f32[12,256,64]{1,2,0:T(8,128)} %convolution_bitcast_fusion) | copy-start | bytes 2359300
  52.4 2.4 %copy-start.16 = (pred[12,2]{1,0:T(8,128)(4,1)S(1)}, pred[12,2]{1,0:T(8,128)(4,1)}, u32[]{:S(2)}) copy-start(pred[12,2]{1,0:T(8,128)(4,1)} %get-tuple-element.18) | copy-start | bytes 76
  52.4 3.7 %copy-start.13 = (f32[12,256,64]{1,2,0:T(8,128)S(1)}, f32[12,256,64]{1,2,0:T(8,128)}, u32[]{:S(2)}) copy-start(f32[12,256,64]{1,2,0:T(8,128)} %fusion.3) | copy-start | bytes 2359300
  52.4 3.7 %copy-start.14 = (f32[12,256,64]{1,2,0:T(8,128)S(1)}, f32[12,256,64]{1,2,0:T(8,128)}, u32[]{:S(2)}) copy-start(f32[12,256,64]{1,2,0:T(8,128)} %convolution_bitcast_fusion.6) | copy-start | bytes 2359300
  54.7 2.2 %copy-start.3 = (bf16[12,16,64,64]{3,2,1,0:T(8,128)(2,1)S(1)}, bf16[12,16,64,64]{3,2,1,0:T(8,128)(2,1)}, u32[]{:S(2)}) copy-start(bf16[12,16,64,64]{3,2,1,0:T(8,128)(2,1)} %reshape.38) | copy-start | bytes 4718596
  54.7 2.5 %copy-start.4 = (bf16[36,64,256]{2,1,0:T(8,128)(2,1)S(1)}, bf16[36,64,256]{2,1,0:T(8,128)(2,1)}, u32[]{:S(2)}) copy-start(bf16[36,64,256]{2,1,0:T(8,128)(2,1)} %gather_fusion.1) | copy-start | bytes 3538948
  55.1 2.6 %copy-start.10 = (bf16[12,256,64]{1,2,0:T(8,128)(2,1)}, bf16[12,256,64]{1,2,0:T(8,128)(2,1)S(1)}, u32[]{:S(2)}) copy-start(bf16[12,256,64]{1,2,0:T(8,128)(2,1)S(1)} %fusion.12) | copy-start | bytes 1179652
  57.2 1.1 copy-start.7
  58.7 132.4 %copy-start.11 = (bf16[12,256,64]{1,2,0:T(8,128)(2,1)}, bf16[12,256,64]{1,2,0:T(8,128)(2,1)S(1)}, u32[]{:S(2)}) copy-start(bf16[12,256,64]{1,2,0:T(8,128)(2,1)S(1)} %fusion.13) | copy-start | bytes 1179652
Sparse Core Ops, SparseCore 0:
  59.8 128.3 all-reduce.2
where the time goes:
time: 198 us
  waiting for transfers between devices  129 us (65%)
  local copies, waits for them, and re-layouts  28.2 us (14%)
  matrix products  16.7 us (8%)
  between operations  14.2 us (7%)
  other arithmetic  5.42 us (3%)
  starting transfers between devices  4.77 us (2%)
    psum x1, waiting for transfers between devices, on_device(): kgram, mgram = lax.psum((kterm, mterm), ('loop', 'grp'))  129 us
    gather x5, local copies, waits for them, and re-layouts, on_device(): picked = blocks[chosen]  13 us
    dot_general x5, matrix products, on_device(): jnp.einsum('rjab,rjbc->rac', mb[:, first:first + count], picked, preferre...  9.93 us
    reshape x1, local copies, waits for them, and re-layouts, on_device(): kb = stiffness.reshape(rows_dev, NB, BS, BS)  5.54 us
    dot_general x5, matrix products, on_device(): jnp.einsum('rjab,rjbc->rac', kb[:, first:first + count], picked, preferre...  4.76 us
    ppermute x3, starting transfers between devices, shifted(): return lax.ppermute(block, axis, route)  4.74 us
    reshape x1, local copies, waits for them, and re-layouts, on_device(): mb = mass.reshape(rows_dev, NB, BS, BS)  4.31 us
  transfers between devices with their start and end apart: 4, of which 1 were waited for; matrix products, arithmetic and copies ran while one was open for 19% of the time, Pallas kernels for 0%

commit v1 on v0

--- a/solution.py
+++ b/solution.py
@@ -55,7 +55,7 @@
     contract = (((0,), (0,)), ((), ()))
     kterm = lax.dot_general(basis, stiff_basis, contract, preferred_element_type=jnp.float32)
     mterm = lax.dot_general(basis, mass_basis, contract, preferred_element_type=jnp.float32)
-    kgram, mgram = lax.psum((kterm, mterm), ("loop", "grp"))
+    kgram, mgram = lax.psum(lax.psum((kterm, mterm), "grp"), "loop")
     total_dofs = basis.shape[0] * lax.axis_size("loop") * lax.axis_size("grp")
     factor = jnp.float32(1.0) / jnp.sqrt(jnp.float32(total_dofs))
     return (stiff_basis, mass_basis, kgram * factor, mgram * factor)

time: 198 us -> 178 us (0.90)
  waiting for transfers between devices: 129 us -> 108 us
    psum x1 -> x2, waiting for transfers between devices: 129 us -> 108 us  [on_device(): kgram, mgram = lax.psum(lax.psum((kterm, mterm), 'grp'), 'loop')]
  transfers between devices with their start and end apart: 4 -> 5, of which waited for: 1 -> 2; matrix products, arithmetic and copies ran while one was open for 19% -> 21% of each run, Pallas kernels for 0% -> 0%
where the time goes in v1:
time: 178 us; the launch traced here: 177 us
  waiting for transfers between devices  108 us (61%)
  local copies, waits for them, and re-layouts  28.2 us (16%)
  matrix products  16.8 us (9%)
  between operations  14.2 us (8%)
  other arithmetic  5.42 us (3%)
  starting transfers between devices  4.81 us (3%)
    psum x2, waiting for transfers between devices, on_device(): kgram, mgram = lax.psum(lax.psum((kterm, mterm), 'grp'), 'loop')  108 us
    gather x5, local copies, waits for them, and re-layouts, on_device(): picked = blocks[chosen]  13 us
    dot_general x5, matrix products, on_device(): jnp.einsum('rjab,rjbc->rac', mb[:, first:first + count], picked, preferre...  9.95 us
    reshape x1, local copies, waits for them, and re-layouts, on_device(): kb = stiffness.reshape(rows_dev, NB, BS, BS)  5.55 us
    dot_general x5, matrix products, on_device(): jnp.einsum('rjab,rjbc->rac', kb[:, first:first + count], picked, preferre...  4.8 us
    ppermute x3, starting transfers between devices, shifted(): return lax.ppermute(block, axis, route)  4.74 us
    reshape x1, local copies, waits for them, and re-layouts, on_device(): mb = mass.reshape(rows_dev, NB, BS, BS)  4.31 us
    unnamed x42, local copies, waits for them, and re-layouts  3.58 us
  transfers between devices with their start and end apart: 5, of which 2 were waited for; matrix products, arithmetic and copies ran while one was open for 21% of the time, Pallas kernels for 0%

profile of v1, /device:TPU:0, one launch (start us, length us, event | category | flops | bytes accessed | tf_op | source)
XLA Modules:
  0.0 177.4 jit_solution(12531716884711763628)
XLA Ops:
  7.2 0.0 all-reduce.5.cloned.1.call-start
  7.2 0.5 collective-permute-start.1
  7.7 2.0 %collective-permute-start = (bf16[768,256]{1,0:T(8,128)(2,1)}, bf16[768,256]{1,0:T(8,128)(2,1)}, u32[]{:S(2)}, u32[]{:S(2)}) collective-permute-start(bf16[768,256]{1,0:T(8,128)(2,1)} %param.5), channel_id=1, source_target_pairs={{8,0},{16,8},{24,16},{0,24},{9,1},{17,9},{25,17},{1,25},{10,2},{18... | collective-permute-start | bytes 1179656 | tf_op jit(solution)/shard_map/ppermute | solution.py:14
  9.7 2.2 %collective-permute-start.2 = (bf16[768,256]{1,0:T(8,128)(2,1)}, bf16[768,256]{1,0:T(8,128)(2,1)}, u32[]{:S(2)}, u32[]{:S(2)}) collective-permute-start(bf16[768,256]{1,0:T(8,128)(2,1)} %param.5), channel_id=1, source_target_pairs={{16,0},{24,8},{0,16},{8,24},{17,1},{25,9},{1,17},{9,25},{18,2},{26... | collective-permute-start | bytes 1179656 | tf_op jit(solution)/shard_map/ppermute | solution.py:14
  11.9 0.8 compare_select_fusion.3
  12.8 0.7 compare_select_fusion.4
  13.5 0.7 iota_compare_fusion
  14.2 0.7 fusion.35
  14.9 0.7 fusion.34
  15.5 0.8 compare_select_fusion.1
  16.4 4.3 %reshape.42 = bf16[12,16,64,64]{3,2,1,0:T(8,128)(2,1)S(1)} reshape(bf16[12,16,4096]{2,1,0:T(8,128)(2,1)} %param.7) | data formatting | bytes 3145728 | tf_op jit(solution)/shard_map/reshape | solution.py:21
  20.7 0.1 reshape.61
  20.8 0.1 reshape.45
  20.9 0.1 reshape.53
  21.0 0.1 reshape.77
  21.1 0.6 pad_clamp_fusion
  21.7 0.1 reshape.69
  21.8 0.6 pad_clamp_fusion.1
  22.4 5.5 %reshape.38 = bf16[12,16,64,64]{3,2,1,0:T(8,128)(2,1)} reshape(bf16[12,16,4096]{2,1,0:T(8,128)(2,1)} %param.6) | data formatting | bytes 3145728 | tf_op jit(solution)/shard_map/reshape | solution.py:20
  27.9 2.4 %gather_fusion = bf16[72,64,256]{2,1,0:T(8,128)(2,1)} fusion(bf16[12,64,256]{2,1,0:T(8,128)(2,1)S(1)} %bitcast.84, s32[1024]{0:T(1024)S(1)} %pad_clamp_fusion.4), kind=kCustom, calls=%fused_computation | custom fusion | bytes 4718880 | tf_op jit(solution)/shard_map/gather | solution.py:37
  30.3 3.4 %fusion.2 = f32[12,256,64]{1,2,0:T(8,128)} fusion(bf16[12,16,64,64]{3,2,1,0:T(8,128)(2,1)S(1)} %reshape.42, bf16[12,6,64,256]{3,2,1,0:T(8,128)(2,1)} %bitcast.91, pred[12,6]{1,0:T(8,128)(4,1)S(1)} %bitcast.99), kind=kOutput, calls=%fused_computation.8 | convolution fusion | flops 152174592 | bytes 4718664 | tf_op jit(solution)/shard_map/rjab,rjbc->rac/dot_general | solution.py:45
  33.7 1.5 fusion.3
  35.2 2.6 %gather_fusion.4 = bf16[24,64,256]{2,1,0:T(8,128)(2,1)} fusion(bf16[12,64,256]{2,1,0:T(8,128)(2,1)} %bitcast.12, s32[1024]{0:T(1024)S(1)} %copy-done.15), kind=kCustom, calls=%fused_computation.4 | custom fusion | bytes 1572960 | tf_op jit(solution)/shard_map/gather | solution.py:37
  37.8 2.6 %gather_fusion.3 = bf16[24,64,256]{2,1,0:T(8,128)(2,1)} fusion(bf16[12,64,256]{2,1,0:T(8,128)(2,1)} %bitcast.12, s32[1024]{0:T(1024)} %pad_clamp_fusion.1), kind=kCustom, calls=%fused_computation.3 | custom fusion | bytes 1572960 | tf_op jit(solution)/shard_map/gather | solution.py:37
  40.4 2.7 %gather_fusion.2 = bf16[36,64,256]{2,1,0:T(8,128)(2,1)} fusion(bf16[12,64,256]{2,1,0:T(8,128)(2,1)} %bitcast.8, s32[1024]{0:T(1024)S(1)} %pad_clamp_fusion.2), kind=kCustom, calls=%fused_computation.2 | custom fusion | bytes 2359440 | tf_op jit(solution)/shard_map/gather | solution.py:37
  43.1 2.7 %convolution_bitcast_fusion.4 = f32[12,256,64]{1,2,0:T(8,128)} fusion(bf16[12,16,64,64]{3,2,1,0:T(8,128)(2,1)S(1)} %reshape.42, bf16[12,3,64,256]{3,2,1,0:T(8,128)(2,1)} %bitcast.97, pred[12,3]{1,0:T(8,128)(4,1)S(1)} %copy-done.19), kind=kOutput, calls=%fused_computation.14 | convolution fusion | flops 76087296 | bytes 3538980 | tf_op jit(solution)/shard_map/rjab,rjbc->rac/dot_general | solution.py:45
  45.9 1.3 convolution_bitcast_fusion
  47.1 1.2 convolution_bitcast_fusion.2
  48.4 1.3 convolution_bitcast_fusion.6
  49.7 2.7 %gather_fusion.1 = bf16[36,64,256]{2,1,0:T(8,128)(2,1)} fusion(bf16[12,64,256]{2,1,0:T(8,128)(2,1)} %bitcast.4, s32[1024]{0:T(1024)S(1)} %pad_clamp_fusion.3), kind=kCustom, calls=%fused_computation.1 | custom fusion | bytes 2359440 | tf_op jit(solution)/shard_map/gather | solution.py:37
  52.4 2.3 %fusion.11 = f32[12,256,64]{1,2,0:T(8,128)S(1)} fusion(f32[12,256,64]{1,2,0:T(8,128)} %convolution_bitcast_fusion.4, f32[12,256,64]{1,2,0:T(8,128)} %fusion.2, bf16[12,16,64,64]{3,2,1,0:T(8,128)(2,1)S(1)} %reshape.42, bf16[12,3,64,256]{3,2,1,0:T(8,128)(2,1)} %bitcast.85, pred[12,3]{1,0:T(8,128)(4,1)S(1)} %copy-done.17), kind=kOutput, calls=%fused_computation.25 | convolution fusion | flops 76480512 | bytes 5111844 | tf_op jit(solution)/shard_map/rjab,rjbc->rac/dot_general | solution.py:45
  54.8 0.3 fusion.12
  55.1 0.0 copy-start.10
  55.1 1.0 convolution_bitcast_fusion.8
  56.1 0.8 copy-done.3
  56.9 0.3 copy-done.4
  57.3 0.4 fusion.9
  57.7 0.7 copy-done.7
  58.4 0.3 fusion.13
  58.8 1.0 convolution_bitcast_fusion.9
  59.8 0.0 all-reduce.5.cloned.1.call-update
  59.8 0.0 all-reduce.7.cloned.1.call-start
  59.8 73.0 %all-reduce.5.cloned.1.call-done = (f32[256,256]{0,1:T(8,128)}, f32[256,256]{0,1:T(8,128)}) async-done(((f32[256,256]{0,1:T(8,128)}, f32[256,256]{0,1:T(8,128)}), (f32[256,256]{0,1:T(8,128)}, f32[256,256]{0,1:T(8,128)})) %all-reduce.5.cloned.1.call-update) | async-done | bytes 524304 | tf_op jit(solution)/shard_map/psum | solution.py:58
  132.9 0.0 all-reduce.7.cloned.1.call-update
  132.9 34.9 %all-reduce.7.cloned.1.call-done = (f32[256,256]{0,1:T(8,128)}, f32[256,256]{0,1:T(8,128)}) async-done(((f32[256,256]{0,1:T(8,128)}, f32[256,256]{0,1:T(8,128)}), (f32[256,256]{0,1:T(8,128)}, f32[256,256]{0,1:T(8,128)})) %all-reduce.7.cloned.1.call-update) | async-done | bytes 524304 | tf_op jit(solution)/shard_map/psum | solution.py:58
  167.8 1.1 broadcast_multiply_fusion
  168.9 0.8 copy.11
  169.7 0.8 copy.12
  (42 shorter events, 0.1 us)
Async XLA Ops:
  7.2 125.7 %all-reduce.5.cloned.1.call-start = ((), (), s32[]{:S(2)}) async-start(), calls=%async_computation | async-start | bytes 1048576 | tf_op jit(solution)/shard_map/psum | solution.py:58
  7.2 33.2 %collective-permute-start.1 = (bf16[768,256]{1,0:T(8,128)(2,1)}, bf16[768,256]{1,0:T(8,128)(2,1)}, u32[]{:S(2)}, u32[]{:S(2)}) collective-permute-start(bf16[768,256]{1,0:T(8,128)(2,1)} %param.5), channel_id=1, source_target_pairs={{24,0},{0,8},{8,16},{16,24},{25,1},{1,9},{9,17},{17,25},{26,2},{2,... | collective-permute-start | bytes 1179656 | tf_op jit(solution)/shard_map/ppermute | solution.py:14
  7.7 42.0 %collective-permute-start = (bf16[768,256]{1,0:T(8,128)(2,1)}, bf16[768,256]{1,0:T(8,128)(2,1)}, u32[]{:S(2)}, u32[]{:S(2)}) collective-permute-start(bf16[768,256]{1,0:T(8,128)(2,1)} %param.5), channel_id=1, source_target_pairs={{8,0},{16,8},{24,16},{0,24},{9,1},{17,9},{25,17},{1,25},{10,2},{18... | collective-permute-start | bytes 1179656 | tf_op jit(solution)/shard_map/ppermute | solution.py:14
  9.7 25.5 %collective-permute-start.2 = (bf16[768,256]{1,0:T(8,128)(2,1)}, bf16[768,256]{1,0:T(8,128)(2,1)}, u32[]{:S(2)}, u32[]{:S(2)}) collective-permute-start(bf16[768,256]{1,0:T(8,128)(2,1)} %param.5), channel_id=1, source_target_pairs={{16,0},{24,8},{0,16},{8,24},{17,1},{25,9},{1,17},{9,25},{18,2},{26... | collective-permute-start | bytes 1179656 | tf_op jit(solution)/shard_map/ppermute | solution.py:14
  22.4 5.6 %copy-start = (bf16[768,256]{1,0:T(8,128)(2,1)S(1)}, bf16[768,256]{1,0:T(8,128)(2,1)}, u32[]{:S(2)}) copy-start(bf16[768,256]{1,0:T(8,128)(2,1)} %param.5) | copy-start | bytes 1179652
  30.3 3.4 %copy-start.1 = (bf16[12,16,64,64]{3,2,1,0:T(8,128)(2,1)S(1)}, bf16[12,16,64,64]{3,2,1,0:T(8,128)(2,1)}, u32[]{:S(2)}) copy-start(bf16[12,16,64,64]{3,2,1,0:T(8,128)(2,1)} %reshape.38) | copy-start | bytes 4718596
  30.3 3.4 %copy-start.9 = (bf16[72,64,256]{2,1,0:T(8,128)(2,1)S(1)}, bf16[72,64,256]{2,1,0:T(8,128)(2,1)}, u32[]{:S(2)}) copy-start(bf16[72,64,256]{2,1,0:T(8,128)(2,1)} %gather_fusion) | copy-start | bytes 7077892
  33.7 1.5 copy-start.15
  37.8 5.4 %copy-start.19 = (pred[12,3]{1,0:T(8,128)(4,1)S(1)}, pred[12,3]{1,0:T(8,128)(4,1)}, u32[]{:S(2)}) copy-start(pred[12,3]{1,0:T(8,128)(4,1)} %get-tuple-element.23) | copy-start | bytes 112
  40.4 5.5 %copy-start.18 = (pred[12,2]{1,0:T(8,128)(4,1)S(1)}, pred[12,2]{1,0:T(8,128)(4,1)}, u32[]{:S(2)}) copy-start(pred[12,2]{1,0:T(8,128)(4,1)} %get-tuple-element.21) | copy-start | bytes 76
  43.1 2.7 %copy-start.6 = (bf16[24,64,256]{2,1,0:T(8,128)(2,1)S(1)}, bf16[24,64,256]{2,1,0:T(8,128)(2,1)}, u32[]{:S(2)}) copy-start(bf16[24,64,256]{2,1,0:T(8,128)(2,1)} %gather_fusion.4) | copy-start | bytes 2359300
  43.1 4.0 %copy-start.2 = (bf16[12,16,64,64]{3,2,1,0:T(8,128)(2,1)S(1)}, bf16[12,16,64,64]{3,2,1,0:T(8,128)(2,1)}, u32[]{:S(2)}) copy-start(bf16[12,16,64,64]{3,2,1,0:T(8,128)(2,1)} %reshape.38) | copy-start | bytes 4718596
  45.9 2.5 %copy-start.12 = (bf16[36,64,256]{2,1,0:T(8,128)(2,1)S(1)}, bf16[36,64,256]{2,1,0:T(8,128)(2,1)}, u32[]{:S(2)}) copy-start(bf16[36,64,256]{2,1,0:T(8,128)(2,1)} %gather_fusion.2) | copy-start | bytes 3538948
  48.4 4.0 %copy-start.17 = (pred[12,3]{1,0:T(8,128)(4,1)S(1)}, pred[12,3]{1,0:T(8,128)(4,1)}, u32[]{:S(2)}) copy-start(pred[12,3]{1,0:T(8,128)(4,1)} %get-tuple-element.22) | copy-start | bytes 112
  52.4 2.3 %copy-start.5 = (bf16[24,64,256]{2,1,0:T(8,128)(2,1)S(1)}, bf16[24,64,256]{2,1,0:T(8,128)(2,1)}, u32[]{:S(2)}) copy-start(bf16[24,64,256]{2,1,0:T(8,128)(2,1)} %gather_fusion.3) | copy-start | bytes 2359300
  52.4 2.3 %copy-start.8 = (f32[12,256,64]{1,2,0:T(8,128)S(1)}, f32[12,256,64]{1,2,0:T(8,128)}, u32[]{:S(2)}) copy-start(f32[12,256,64]{1,2,0:T(8,128)} %convolution_bitcast_fusion) | copy-start | bytes 2359300
  52.4 2.4 %copy-start.16 = (pred[12,2]{1,0:T(8,128)(4,1)S(1)}, pred[12,2]{1,0:T(8,128)(4,1)}, u32[]{:S(2)}) copy-start(pred[12,2]{1,0:T(8,128)(4,1)} %get-tuple-element.20) | copy-start | bytes 76
  52.4 3.7 %copy-start.13 = (f32[12,256,64]{1,2,0:T(8,128)S(1)}, f32[12,256,64]{1,2,0:T(8,128)}, u32[]{:S(2)}) copy-start(f32[12,256,64]{1,2,0:T(8,128)} %fusion.3) | copy-start | bytes 2359300
  52.4 3.7 %copy-start.14 = (f32[12,256,64]{1,2,0:T(8,128)S(1)}, f32[12,256,64]{1,2,0:T(8,128)}, u32[]{:S(2)}) copy-start(f32[12,256,64]{1,2,0:T(8,128)} %convolution_bitcast_fusion.6) | copy-start | bytes 2359300
  54.7 2.2 %copy-start.3 = (bf16[12,16,64,64]{3,2,1,0:T(8,128)(2,1)S(1)}, bf16[12,16,64,64]{3,2,1,0:T(8,128)(2,1)}, u32[]{:S(2)}) copy-start(bf16[12,16,64,64]{3,2,1,0:T(8,128)(2,1)} %reshape.38) | copy-start | bytes 4718596
  54.7 2.5 %copy-start.4 = (bf16[36,64,256]{2,1,0:T(8,128)(2,1)S(1)}, bf16[36,64,256]{2,1,0:T(8,128)(2,1)}, u32[]{:S(2)}) copy-start(bf16[36,64,256]{2,1,0:T(8,128)(2,1)} %gather_fusion.1) | copy-start | bytes 3538948
  55.1 2.6 %copy-start.10 = (bf16[12,256,64]{1,2,0:T(8,128)(2,1)}, bf16[12,256,64]{1,2,0:T(8,128)(2,1)S(1)}, u32[]{:S(2)}) copy-start(bf16[12,256,64]{1,2,0:T(8,128)(2,1)S(1)} %fusion.12) | copy-start | bytes 1179652
  57.3 1.1 copy-start.7
  58.7 111.8 %copy-start.11 = (bf16[12,256,64]{1,2,0:T(8,128)(2,1)}, bf16[12,256,64]{1,2,0:T(8,128)(2,1)S(1)}, u32[]{:S(2)}) copy-start(bf16[12,256,64]{1,2,0:T(8,128)(2,1)S(1)} %fusion.13) | copy-start | bytes 1179652
  59.8 108.0 %all-reduce.7.cloned.1.call-start = ((), (), s32[]{:S(2)}) async-start(), calls=%async_computation.1 | async-start | bytes 1048576 | tf_op jit(solution)/shard_map/psum | solution.py:58
Sparse Core Ops, SparseCore 0:
  59.9 72.9 all-reduce.4
  135.4 32.3 all-reduce.6
